TPU v7x, 128 devices: a whole 4x4x4 slice. The times are simulated.
128 devices in a mesh: row: 4 (over y), col: 32 (over x, z, core).
Axes of the slice: x: 4, y: 4, z: 4, core: 2. Of those that a mesh axis runs over, the one named last changes fastest.
Arguments:
- charges: float32 [16, 32, 16, 256], P('row', 'col'), may hold values from -6 to 6
- column_order: int32 [32], replicated, may hold values from 0 to 31, as said below
- vertices: float32 [3, 66177], replicated, as said below
- panel_vertices: int32 [3, 131072], replicated, may hold values from 0 to 66176, as said below
- near_pairs: int32 [2, 2048], replicated, may hold values from 0 to 511, as said below
Outputs:
- potential_one: float32 [16, 32, 16, 256], P('row', 'col')
- potential_two: float32 [16, 32, 16, 256], P('row', 'col')
Inputs may be any that keep to these rules, and one draw needn't show every extreme that they name: column_order is a permutation of 0 to 31. `panel_vertices`: panels b * 256 to (b + 1) * 256 - 1 cover block b, a patch of 8 x 16 lattice quads each cut into two triangles along one of its diagonals; vertex ids are lattice row * 513 + lattice column. `vertices`: a jittered lattice of spacing 1.8 in x and y with heights in z; every panel has positive area. `near_pairs`: each column is a pair of distinct block ids, lower first, listed once; the higher block lies at most 3 grid rows below and within squared grid distance 12 of the lower one; entries 512 * b to 512 * (b + 1) - 1 are exactly the pairs whose lower block lies in grid rows 4 * b to 4 * (b + 1) - 1.
All inputs are finite; a program needn't handle non-finite values.
Results may differ from a plain program's by a relative error of at most 0.0003.
Values sent between devices are 32-bit elements; how exact they have to be, the bound alone decides.
A program may use at most 320 MiB of HBM per device.

v0:
```python
import math
import jax
import jax.numpy as jnp
import numpy as np
from jax import lax
from jax.sharding import PartitionSpec as P

PANELS = 256
REACH = 4


def shifted(value, axis, by):
    length = lax.axis_size(axis)
    pairs = [(i, i + by) for i in range(length) if 0 <= i + by < length]
    return lax.ppermute(value, axis, pairs)


def rule_tables():
    gauss_two = np.array([-1.0, 1.0]) / math.sqrt(3.0)
    gauss_four = np.array(
        [-0.8611363115940526, -0.3399810435848563, 0.3399810435848563, 0.8611363115940526]
    )
    weight_four = np.array(
        [0.3478548451374538, 0.6521451548625461, 0.6521451548625461, 0.3478548451374538]
    )
    corner_weights = []
    point_weights = []
    for first_index in range(2):
        for second_index in range(4):
            along = 0.5 * (1.0 + gauss_two[first_index])
            across = 0.5 * (1.0 + gauss_four[second_index])
            corner_weights.append([along, (1.0 - along) * across, (1.0 - along) * (1.0 - across)])
            point_weights.append(2.0 * 0.5 * 0.5 * weight_four[second_index] * (1.0 - along))
    return (np.array(corner_weights), np.array(point_weights))


def block_geometry(vertices, panel_vertices, block_ids):
    panels = panel_vertices.reshape(3, -1, PANELS)[:, block_ids]
    corners = jnp.transpose(vertices[:, panels], (2, 1, 0, 3))
    centre = (corners[:, 0] + corners[:, 1] + corners[:, 2]) / 3.0
    first_edge = corners[:, 1] - corners[:, 0]
    second_edge = corners[:, 2] - corners[:, 0]
    normal_x = first_edge[:, 1] * second_edge[:, 2] - first_edge[:, 2] * second_edge[:, 1]
    normal_y = first_edge[:, 2] * second_edge[:, 0] - first_edge[:, 0] * second_edge[:, 2]
    normal_z = first_edge[:, 0] * second_edge[:, 1] - first_edge[:, 1] * second_edge[:, 0]
    panel_area = 0.5 * jnp.sqrt(normal_x * normal_x + normal_y * normal_y + normal_z * normal_z)
    corner_weights, _ = rule_tables()
    points = jnp.einsum(
        "kc,gcxp->gxkp",
        jnp.asarray(corner_weights, corners.dtype),
        corners,
        precision=lax.Precision.HIGHEST,
    )
    return (centre, points, panel_area)


def tile_block(target, source):
    target_centre, target_points, target_area = target
    source_centre, source_points, source_area = source
    _, point_weights = rule_tables()
    kernel_sum = jnp.zeros(
        (target_centre.shape[0], target_centre.shape[2], source_centre.shape[2]), jnp.float32
    )
    for point_index in range(8):
        weight = float(point_weights[point_index])
        distance = target_centre[:, :, :, None] - source_points[:, :, point_index, None, :]
        kernel_sum = kernel_sum + weight * lax.rsqrt(jnp.sum(distance * distance, axis=1) + 0.01)
        distance = target_points[:, :, point_index, :, None] - source_centre[:, :, None, :]
        kernel_sum = kernel_sum + weight * lax.rsqrt(jnp.sum(distance * distance, axis=1) + 0.01)
    return kernel_sum * target_area[:, :, None] * source_area[:, None, :] / (8.0 * math.pi)


def apply_tiles(source_values, tile_stack):
    return jnp.einsum("grq,gpq->grp", source_values, tile_stack, precision=lax.Precision.HIGHEST)


def apply_transposed(source_values, tile_stack):
    return jnp.einsum("grp,gpq->grq", source_values, tile_stack, precision=lax.Precision.HIGHEST)


def prepare(column_order, vertices, panel_vertices, near_pairs, band_rows):
    columns = lax.axis_size("col")
    band_count = lax.axis_size("row")
    band_index = lax.axis_index("row")
    column_index = lax.axis_index("col")
    positions = jnp.arange(columns, dtype=jnp.int32)
    position_of = jnp.sum(
        jnp.where(column_order[:, None] == positions[None, :], positions[:, None], 0), axis=0
    )
    home_column = jnp.sum(jnp.where(positions == column_index, column_order, 0))
    first_row = band_index * band_rows
    own_blocks = (first_row + jnp.arange(band_rows, dtype=jnp.int32)) * columns + home_column
    band_pairs = near_pairs.shape[1] // band_count
    share = band_pairs // columns
    segment = lax.dynamic_slice_in_dim(
        near_pairs, band_index * band_pairs + column_index * share, share, 1
    )
    low_blocks = segment[0]
    high_blocks = segment[1]
    targets = jnp.concatenate([own_blocks, low_blocks])
    sources = jnp.concatenate([own_blocks, high_blocks])
    tiles = tile_block(
        block_geometry(vertices, panel_vertices, targets),
        block_geometry(vertices, panel_vertices, sources),
    )
    self_tiles = tiles[:band_rows]
    pair_tiles = tiles[band_rows:]
    low_row = low_blocks // columns - first_row
    high_row = high_blocks // columns - first_row
    low_pos = position_of[low_blocks % columns]
    high_pos = position_of[high_blocks % columns]
    slot_table = (low_row, low_pos, high_row, high_pos)
    return (self_tiles, pair_tiles, slot_table)


def near_product(block_values, prepared):
    self_tiles, pair_tiles, slot_table = prepared
    band_rows = block_values.shape[0]
    low_row, low_pos, high_row, high_pos = slot_table
    self_term = apply_tiles(block_values[:, 0], self_tiles)
    later = shifted(block_values[:REACH], "row", -1)
    source_table = lax.all_gather(
        jnp.concatenate([block_values, later], axis=0), "col", axis=1, tiled=True
    )
    to_low = apply_tiles(source_table[high_row, high_pos], pair_tiles)
    to_high = apply_transposed(source_table[low_row, low_pos], pair_tiles)
    partial_value = jnp.zeros(source_table.shape, jnp.float32)
    partial_value = (
        partial_value.at[low_row, low_pos].add(to_low).at[high_row, high_pos].add(to_high)
    )
    summed = lax.psum_scatter(partial_value, "col", scatter_dimension=1, tiled=True)
    carried_down = shifted(summed[band_rows:], "row", 1)
    head = summed[:REACH] + carried_down
    own = jnp.concatenate([head, summed[REACH:band_rows]], axis=0)
    return own + self_term[:, None]


def body(charges, column_order, vertices, panel_vertices, near_pairs):
    prepared = prepare(column_order, vertices, panel_vertices, near_pairs, charges.shape[0])
    potential_one = near_product(charges, prepared)
    potential_two = near_product(potential_one, prepared)
    return (potential_one, potential_two)


def solution(mesh):
    return jax.shard_map(
        body,
        mesh=mesh,
        in_specs=(P("row", "col", None, None), P(), P(), P(), P()),
        out_specs=(P("row", "col", None, None), P("row", "col", None, None)),
        check_vma=False,
    )
```

profile of v0, /device:TPU:8, one launch (start us, length us, event | category | flops | bytes accessed | tf_op | source)
XLA Modules:
  0.0 580.7 jit_solution(6145317578535073538)
XLA Ops:
  7.2 0.0 all-gather.3.cloned.1.call-start
  7.2 2.4 collective-permute-start
  9.7 0.8 constant_dynamic-slice_fusion
  10.4 1.3 fusion.42
  11.7 0.7 select_reduce_fusion
  12.5 0.7 add_bitcast_fusion
  13.1 0.1 fusion.45
  13.2 0.6 gather_fusion.5
  13.9 16.3 %copy.111 = f32[3,66177]{0,1:T(8,128)} copy(f32[3,66177]{1,0:T(4,128)} %param.9) | data formatting | bytes 1588248 | tf_op args[2]
  30.2 62.1 %gather_fusion.6 = f32[15360,3]{1,0:T(8,128)} fusion(f32[3,66177]{0,1:T(8,128)} %copy.111, s32[15360]{0:T(1024)S(1)} %broadcast_clamp_fusion), kind=kCustom, calls=%fused_computation.6 | custom fusion | bytes 430080 | tf_op jit(solution)/shard_map/gather | solution.py:39
  92.3 5.7 copy.117
  97.9 0.6 convolution_bitcast_fusion.1
  98.5 0.3 fusion.51
  98.9 0.6 gather_fusion.3
  99.6 62.1 %gather_fusion.4 = f32[15360,3]{1,0:T(8,128)} fusion(f32[3,66177]{0,1:T(8,128)} %copy.111, s32[15360]{0:T(1024)S(1)} %broadcast_clamp_fusion.1), kind=kCustom, calls=%fused_computation.4 | custom fusion | bytes 430080 | tf_op jit(solution)/shard_map/gather | solution.py:39
  161.7 5.3 copy.112
  167.1 5.7 copy.120
  172.7 0.6 convolution_bitcast_fusion
  173.3 0.3 fusion.52
  173.7 5.3 copy.116
  179.0 0.7 gather_fusion.1
  179.8 0.7 gather_fusion
  181.6 0.6 pad_maximum_fusion
  182.2 0.0 all-gather.3.cloned.1.call-update
  182.2 0.2 reduce-scatter.3.cloned.1.call-start
  182.5 34.1 %multiply_reduce_fusion.15 = (f32[20,256,256]{2,1,0:T(8,128)}, f32[20,256,256]{2,1,0:T(8,128)}, f32[20,256,256]{2,1,0:T(8,128)}, f32[20,256,256]{2,1,0:T(8,128)}...) fusion(f32[20,3,256]{2,1,0:T(4,128)S(1)} %copy.119, ...), kind=kLoop, calls=%fused_computation.29 | loop fusion | flops 83886080 | bytes 42496000 | tf_op jit(solution)/shard_map/reduce_sum | solution.py:67
  216.5 33.9 %multiply_reduce_fusion.14 = (f32[20,256,256]{2,1,0:T(8,128)}, f32[20,256,256]{2,1,0:T(8,128)}, f32[20,256,256]{2,1,0:T(8,128)}, f32[20,256,256]{2,1,0:T(8,128)}...) fusion(f32[20,3,256]{2,1,0:T(4,128)S(1)} %copy.123, ...), kind=kLoop, calls=%fused_computation.28 | loop fusion | flops 83886080 | bytes 42496000 | tf_op jit(solution)/shard_map/reduce_sum | solution.py:69
  250.5 29.1 %fusion.15 = f32[20,256,256]{2,1,0:T(8,128)} fusion(f32[20,256,256]{2,1,0:T(8,128)} %get-tuple-element.25, f32[20,256,256]{2,1,0:T(8,128)} %get-tuple-element.17, f32[20,256,256]{2,1,0:T(8,128)} %get-tuple-element.24, f32[20,256,256]{2,1,0:T(8,128)} %get-tuple-element.16, f32[20,256,256]{2,1,0:T(8,128)} %get-tuple-element.23, ...), kind=kLoop, calls=%fused_computation.46 | loop fusion | flops 64225280 | bytes 89169920 | tf_op jit(solution)/shard_map/div | solution.py:70
  279.6 0.0 all-gather.3.cloned.1.call-done
  279.6 2.8 gather_fusion.2
  282.4 5.7 fusion.22
  288.0 2.8 gather_fusion.7
  290.8 4.3 fusion.20
  295.1 2.6 broadcast.447.clone
  297.7 2.7 scatter_fusion
  300.5 2.6 scatter_fusion.1
  303.0 4.8 copy.152
  307.9 0.0 reduce-scatter.3.cloned.1.call-update
  307.9 0.0 all-gather.5.cloned.1.call-start
  307.9 84.7 %reduce-scatter.3.cloned.1.call-done = f32[8,1,16,256]{3,2,0,1:T(8,128)} async-done(((f32[8,32,16,256]{3,2,0,1:T(8,128)}), f32[8,1,16,256]{3,2,0,1:T(8,128)}) %reduce-scatter.3.cloned.1.call-update) | async-done | bytes 131088 | tf_op jit(solution)/shard_map/reduce_scatter | solution.py:131
  392.6 0.8 slice.252
  393.4 3.4 collective-permute-start.1
  396.9 2.7 collective-permute-done.1
  399.6 2.2 fusion.31
  401.8 1.9 collective-permute-start.2
  403.7 4.2 collective-permute-done.2
  408.0 0.7 pad_maximum_fusion.1
  408.6 0.0 all-gather.5.cloned.1.call-update
  408.6 0.3 reduce-scatter.5.cloned.1.call-start
  409.0 45.5 %all-gather.5.cloned.1.call-done = f32[8,32,16,256]{3,2,0,1:T(8,128)} async-done(((f32[8,1,16,256]{3,2,0,1:T(8,128)}), f32[8,32,16,256]{3,2,0,1:T(8,128)}) %all-gather.5.cloned.1.call-update) | async-done | bytes 4194320 | tf_op jit(solution)/shard_map/all_gather | solution.py:122
  454.4 2.8 gather_fusion.9
  457.2 4.3 fusion.16
  461.5 2.8 gather_fusion.8
  464.3 5.7 fusion.18
  470.0 2.6 broadcast.447
  472.6 2.7 scatter_fusion.2
  475.3 2.6 scatter_fusion.3
  477.9 4.8 copy.153
  482.8 0.0 reduce-scatter.5.cloned.1.call-update
  482.8 81.5 %reduce-scatter.5.cloned.1.call-done = f32[8,1,16,256]{3,2,0,1:T(8,128)} async-done(((f32[8,32,16,256]{3,2,0,1:T(8,128)}), f32[8,1,16,256]{3,2,0,1:T(8,128)}) %reduce-scatter.5.cloned.1.call-update) | async-done | bytes 131088 | tf_op jit(solution)/shard_map/reduce_scatter | solution.py:131
  564.3 0.8 slice.254
  565.2 3.4 collective-permute-start.3
  568.6 2.7 collective-permute-done.3
  571.3 2.8 fusion.30
  (68 shorter events, 1.1 us)
Async XLA Ops:
  7.2 6.0 %copy-start = (s32[3,131072]{1,0:T(4,128)S(1)}, s32[3,131072]{1,0:T(4,128)}, u32[]{:S(2)}) copy-start(s32[3,131072]{1,0:T(4,128)} %param.10) | copy-start | bytes 4718596
  7.2 272.4 %all-gather.3.cloned.1.call-start = ((), (), s32[]{:S(2)}) async-start(), calls=%async_computation.2 | async-start | bytes 4325376 | tf_op jit(solution)/shard_map/all_gather | solution.py:122
  7.2 174.3 %collective-permute-start = (f32[4,1,16,256]{3,2,1,0:T(8,128)}, f32[4,1,16,256]{3,2,1,0:T(8,128)S(1)}, u32[]{:S(2)}, u32[]{:S(2)}) collective-permute-start(f32[4,1,16,256]{3,2,1,0:T(8,128)} %param.7), channel_id=1, source_target_pairs={{32,0},{64,32},{96,64},{33,1},{65,33},{97,65},{34,2},{66,34},{98,6... | collective-permute-start | bytes 196616 | tf_op jit(solution)/shard_map/ppermute | solution.py:15
  30.2 67.7 %copy-start.5 = (f32[8,3,1,1]{0,1,3,2:T(4,128)S(1)}, f32[8,3,1,1]{0,1,3,2:T(4,128)}, u32[]{:S(2)}) copy-start(f32[8,3,1,1]{0,1,3,2:T(4,128)} %constant.210) | copy-start | bytes 292
  179.0 2.6 copy-start.4
  182.2 210.4 %reduce-scatter.3.cloned.1.call-start = ((), (), s32[]{:S(2)}) async-start(), calls=%async_computation.3 | async-start | bytes 4325376 | tf_op jit(solution)/shard_map/reduce_scatter | solution.py:131
  216.5 33.9 %copy-start.2 = (f32[20,256,256]{2,1,0:T(8,128)S(1)}, f32[20,256,256]{2,1,0:T(8,128)}, u32[]{:S(2)}) copy-start(f32[20,256,256]{2,1,0:T(8,128)} %get-tuple-element.10) | copy-start | bytes 15728644
  307.9 146.6 %all-gather.5.cloned.1.call-start = ((), (), s32[]{:S(2)}) async-start(), calls=%async_computation.4 | async-start | bytes 4325376 | tf_op jit(solution)/shard_map/all_gather | solution.py:122
  393.4 6.1 %collective-permute-start.1 = (f32[4,1,16,256]{3,2,0,1:T(8,128)S(1)}, f32[4,1,16,256]{3,2,0,1:T(8,128)S(1)}, u32[]{:S(2)}, u32[]{:S(2)}) collective-permute-start(f32[4,1,16,256]{3,2,0,1:T(8,128)S(1)} %slice.252), channel_id=1, source_target_pairs={{0,32},{32,64},{64,96},{1,33},{33,65},{65,97},{2,34},{34,66},{66,9... | collective-permute-start | bytes 196616 | tf_op jit(solution)/shard_map/ppermute | solution.py:15
  401.8 169.5 %copy-start.3 = (f32[4,1,16,256]{3,2,0,1:T(8,128)}, f32[4,1,16,256]{3,2,0,1:T(8,128)S(1)}, u32[]{:S(2)}) copy-start(f32[4,1,16,256]{3,2,0,1:T(8,128)S(1)} %fusion.31) | copy-start | bytes 196612
  401.8 6.2 %collective-permute-start.2 = (f32[4,1,16,256]{3,2,0,1:T(8,128)S(1)}, f32[4,1,16,256]{3,2,0,1:T(8,128)S(1)}, u32[]{:S(2)}, u32[]{:S(2)}) collective-permute-start(f32[4,1,16,256]{3,2,0,1:T(8,128)S(1)} %fusion.31), channel_id=1, source_target_pairs={{32,0},{64,32},{96,64},{33,1},{65,33},{97,65},{34,2},{66,34},{98,6... | collective-permute-start | bytes 196616 | tf_op jit(solution)/shard_map/ppermute | solution.py:15
  408.6 155.7 %reduce-scatter.5.cloned.1.call-start = ((), (), s32[]{:S(2)}) async-start(), calls=%async_computation.5 | async-start | bytes 4325376 | tf_op jit(solution)/shard_map/reduce_scatter | solution.py:131
  475.3 98.8 %copy-start.1 = (s32[3,131072]{1,0:T(4,128)S(1)}, s32[3,131072]{1,0:T(4,128)}, u32[]{:S(2)}) copy-start(s32[3,131072]{1,0:T(4,128)} %param.10) | copy-start | bytes 4718596
  565.2 6.1 %collective-permute-start.3 = (f32[4,1,16,256]{3,2,0,1:T(8,128)S(1)}, f32[4,1,16,256]{3,2,0,1:T(8,128)S(1)}, u32[]{:S(2)}, u32[]{:S(2)}) collective-permute-start(f32[4,1,16,256]{3,2,0,1:T(8,128)S(1)} %slice.254), channel_id=1, source_target_pairs={{0,32},{32,64},{64,96},{1,33},{33,65},{65,97},{2,34},{34,66},{66,9... | collective-permute-start | bytes 196616 | tf_op jit(solution)/shard_map/ppermute | solution.py:15
Sparse Core Ops, SparseCore 0:
  182.3 48.8 all-gather.2
  308.0 84.5 reduce-scatter.2
  408.8 45.6 all-gather.4
  482.9 81.3 reduce-scatter.4
where the time goes:
time: 582 us; the launch traced here: 581 us
  waiting for transfers between devices  221 us (38%)
  local copies, waits for them, and re-layouts  195 us (34%)
  other arithmetic  112 us (19%)
  matrix products  26.2 us (5%)
  between operations  14.4 us (2%)
  starting transfers between devices  11.8 us (2%)
    reduce_scatter x2, waiting for transfers between devices, near_product(): lax.psum_scatter(partial_value, 'col', scatter_dimension=1, tiled=True)  166 us
    gather x4, local copies, waits for them, and re-layouts, block_geometry(): corners = jnp.transpose(vertices[:, panels], (2, 1, 0, 3))  135 us
    reduce_sum x2, other arithmetic, tile_block(): jnp.sum(distance * distance, axis=1) + 0.01  68 us
    all_gather x2, waiting for transfers between devices, near_product(): lax.all_gather(jnp.concatenate([block_values, later], axis=0), 'col', axi...  45.5 us
    div x1, other arithmetic, tile_block(): kernel_sum * target_area[:, :, None] * source_area[:, None, :]  29.1 us
    dot_general x4, matrix products, apply_tiles(): jnp.einsum('grq,gpq->grp', source_values, tile_stack, precision=lax.Preci...  16.4 us
    unnamed x13, local copies, waits for them, and re-layouts  16.3 us
  transfers between devices with their start and end apart: 8, of which 6 were waited for; matrix products, arithmetic and copies ran while one was open for 46% of the time, Pallas kernels for 0%

commit v1 on v0

--- a/solution.py
+++ b/solution.py
@@ -119,9 +119,13 @@
     low_row, low_pos, high_row, high_pos = slot_table
     self_term = apply_tiles(block_values[:, 0], self_tiles)
     later = shifted(block_values[:REACH], "row", -1)
-    source_table = lax.all_gather(
-        jnp.concatenate([block_values, later], axis=0), "col", axis=1, tiled=True
-    )
+    u = jnp.concatenate([block_values, later], axis=0)
+    by_rank = []
+    for _ in range(jax.lax.axis_size("col")):
+        by_rank.append(u)
+    new = jnp.stack(by_rank, 0)
+    side_arr = jax.lax.all_to_all(new, axis_name="col", split_axis=0, concat_axis=0)
+    source_table = jnp.concatenate(side_arr, axis=1)
     to_low = apply_tiles(source_table[high_row, high_pos], pair_tiles)
     to_high = apply_transposed(source_table[low_row, low_pos], pair_tiles)
     partial_value = jnp.zeros(source_table.shape, jnp.float32)

time: 582 us -> 625 us (1.074)
  blocking collectives: 0 us -> 55.6 us
  waiting for transfers between devices: 221 us -> 195 us
  starting transfers between devices: 11.8 us -> 19.6 us
    all_to_all x0 -> x1, blocking collectives: none -> 55.6 us  [near_product(): jax.lax.all_to_all(new, axis_name='col', split_axis=0, concat_axis=0)]
    all_gather x2 -> x0, waiting for transfers between devices: 45.5 us -> none  [near_product(): lax.all_gather(jnp.concatenate([block_values, later], axis=0), 'col', axi...]
    all_to_all x0 -> x1, waiting for transfers between devices: none -> 22.1 us  [near_product(): jax.lax.all_to_all(new, axis_name='col', split_axis=0, concat_axis=0)]
    all_to_all x0 -> x1, starting transfers between devices: none -> 8.38 us  [near_product(): jax.lax.all_to_all(new, axis_name='col', split_axis=0, concat_axis=0)]
    unnamed x13 -> x11, local copies, waits for them, and re-layouts: 16.3 us -> 16.3 us
  transfers between devices with their start and end apart: 8 -> 7, of which waited for: 6 -> 6; matrix products, arithmetic and copies ran while one was open for 46% -> 44% of each run, Pallas kernels for 0% -> 0%
where the time goes in v1:
time: 625 us; the launch traced here: 623 us
  local copies, waits for them, and re-layouts  198 us (32%)
  waiting for transfers between devices  195 us (31%)
  other arithmetic  114 us (18%)
  blocking collectives  55.6 us (9%)
  matrix products  26.2 us (4%)
  starting transfers between devices  19.6 us (3%)
  between operations  14.6 us (2%)
    reduce_scatter x2, waiting for transfers between devices, near_product(): lax.psum_scatter(partial_value, 'col', scatter_dimension=1, tiled=True)  163 us
    gather x4, local copies, waits for them, and re-layouts, block_geometry(): corners = jnp.transpose(vertices[:, panels], (2, 1, 0, 3))  135 us
    reduce_sum x2, other arithmetic, tile_block(): jnp.sum(distance * distance, axis=1) + 0.01  69.3 us
    all_to_all x1, blocking collectives, near_product(): jax.lax.all_to_all(new, axis_name='col', split_axis=0, concat_axis=0)  55.6 us
    div x1, other arithmetic, tile_block(): kernel_sum * target_area[:, :, None] * source_area[:, None, :]  30.6 us
    all_to_all x1, waiting for transfers between devices, near_product(): jax.lax.all_to_all(new, axis_name='col', split_axis=0, concat_axis=0)  22.1 us
    dot_general x4, matrix products, apply_tiles(): jnp.einsum('grq,gpq->grp', source_values, tile_stack, precision=lax.Preci...  16.4 us
    unnamed x11, local copies, waits for them, and re-layouts  16.3 us
  transfers between devices with their start and end apart: 7, of which 6 were waited for; matrix products, arithmetic and copies ran while one was open for 44% of the time, Pallas kernels for 0%

profile of v1, /device:TPU:8, one launch (start us, length us, event | category | flops | bytes accessed | tf_op | source)
XLA Modules:
  0.0 623.0 jit_solution(16655237711972097711)
XLA Ops:
  7.2 0.0 copy-start
  7.2 2.4 collective-permute-start
  9.6 0.8 constant_dynamic-slice_fusion
  10.4 1.3 fusion.42
  11.7 0.7 select_reduce_fusion
  12.4 0.7 add_bitcast_fusion
  13.1 0.1 fusion.45
  13.2 0.6 gather_fusion.5
  13.9 16.3 %copy.65 = f32[3,66177]{0,1:T(8,128)} copy(f32[3,66177]{1,0:T(4,128)} %param.9) | data formatting | bytes 1588248 | tf_op args[2]
  30.1 62.1 %gather_fusion.6 = f32[15360,3]{1,0:T(8,128)} fusion(f32[3,66177]{0,1:T(8,128)} %copy.65, s32[15360]{0:T(1024)S(1)} %broadcast_clamp_fusion), kind=kCustom, calls=%fused_computation.6 | custom fusion | bytes 430080 | tf_op jit(solution)/shard_map/gather | solution.py:39
  92.2 5.7 copy.71
  97.9 0.6 convolution_bitcast_fusion.1
  98.5 0.3 fusion.51
  99.3 0.6 gather_fusion.3
  100.0 62.1 %gather_fusion.4 = f32[15360,3]{1,0:T(8,128)} fusion(f32[3,66177]{0,1:T(8,128)} %copy.65, s32[15360]{0:T(1024)S(1)} %broadcast_clamp_fusion.1), kind=kCustom, calls=%fused_computation.4 | custom fusion | bytes 430080 | tf_op jit(solution)/shard_map/gather | solution.py:39
  162.1 5.3 copy.66
  167.5 5.7 copy.74
  173.2 0.6 convolution_bitcast_fusion
  173.8 0.3 fusion.52
  174.6 5.3 copy.70
  180.0 0.7 gather_fusion.1
  180.7 0.7 gather_fusion
  181.5 35.4 %multiply_reduce_fusion.15 = (f32[20,256,256]{2,1,0:T(8,128)}, f32[20,256,256]{2,1,0:T(8,128)}, f32[20,256,256]{2,1,0:T(8,128)}, f32[20,256,256]{2,1,0:T(8,128)}...) fusion(f32[20,3,256]{2,1,0:T(4,128)S(1)} %copy.73, ...), kind=kLoop, calls=%fused_computation.29 | loop fusion | flops 83886080 | bytes 42496000 | tf_op jit(solution)/shard_map/reduce_sum | solution.py:67
  216.9 33.9 %multiply_reduce_fusion.14 = (f32[20,256,256]{2,1,0:T(8,128)}, f32[20,256,256]{2,1,0:T(8,128)}, f32[20,256,256]{2,1,0:T(8,128)}, f32[20,256,256]{2,1,0:T(8,128)}...) fusion(f32[20,3,256]{2,1,0:T(4,128)S(1)} %copy.77, ...), kind=kLoop, calls=%fused_computation.28 | loop fusion | flops 83886080 | bytes 42496000 | tf_op jit(solution)/shard_map/reduce_sum | solution.py:69
  250.8 0.0 collective-permute-done
  250.9 2.7 stack.4
  253.5 8.4 %all-to-all-start = ((f32[32,8,1,16,256]{4,3,2,1,0:T(8,128)}), f32[32,8,1,16,256]{4,3,2,1,0:T(8,128)}, u32[]{:S(2)}, u32[]{:S(2)}) async-start(f32[32,8,1,16,256]{4,3,2,1,0:T(8,128)} %stack.4), calls=%async_computation | async-start | bytes 8388608 | tf_op jit(solution)/shard_map/all_to_all | solution.py:127
  261.9 0.0 reduce-scatter.3.cloned.1.call-start
  261.9 30.6 %fusion.15 = f32[20,256,256]{2,1,0:T(8,128)} fusion(f32[20,256,256]{2,1,0:T(8,128)} %get-tuple-element.23, f32[20,256,256]{2,1,0:T(8,128)} %get-tuple-element.15, f32[20,256,256]{2,1,0:T(8,128)} %get-tuple-element.22, f32[20,256,256]{2,1,0:T(8,128)} %get-tuple-element.14, f32[20,256,256]{2,1,0:T(8,128)} %get-tuple-element.21, ...), kind=kLoop, calls=%fused_computation.46 | loop fusion | flops 64225280 | bytes 89169920 | tf_op jit(solution)/shard_map/div | solution.py:70
  292.5 22.1 %all-to-all-done = f32[32,8,1,16,256]{4,3,2,1,0:T(8,128)} async-done(((f32[32,8,1,16,256]{4,3,2,1,0:T(8,128)}), f32[32,8,1,16,256]{4,3,2,1,0:T(8,128)}, u32[]{:S(2)}, u32[]{:S(2)}) %all-to-all-start) | async-done | bytes 4194336 | tf_op jit(solution)/shard_map/all_to_all | solution.py:127
  314.7 2.8 gather_fusion.7
  317.5 2.8 gather_fusion.2
  320.2 4.3 fusion.20
  324.5 5.7 fusion.22
  330.2 2.6 broadcast.453.clone
  332.8 2.7 scatter_fusion
  335.5 2.6 scatter_fusion.1
  338.1 4.8 copy.106
  342.9 0.0 reduce-scatter.3.cloned.1.call-update
  343.0 0.0 reduce-scatter.5.cloned.1.call-start
  343.0 83.0 %reduce-scatter.3.cloned.1.call-done = f32[8,1,16,256]{3,2,0,1:T(8,128)} async-done(((f32[8,32,16,256]{3,2,0,1:T(8,128)}), f32[8,1,16,256]{3,2,0,1:T(8,128)}) %reduce-scatter.3.cloned.1.call-update) | async-done | bytes 131088 | tf_op jit(solution)/shard_map/reduce_scatter | solution.py:135
  426.0 0.8 slice.252
  426.8 3.4 collective-permute-start.1
  430.2 2.7 collective-permute-done.1
  433.0 2.2 fusion.31
  435.2 0.0 copy-start.2
  435.2 1.9 collective-permute-start.2
  437.1 4.2 collective-permute-done.2
  441.4 0.5 stack.5
  441.9 55.6 %all_to_all.10 = f32[32,8,1,16,256]{4,3,2,1,0:T(8,128)} all-to-all(f32[32,8,1,16,256]{4,3,2,1,0:T(8,128)S(1)} %stack.5), channel_id=1, replica_groups=mesh['row'=4,'col'=32] {'col'}, dimensions={0} | all-to-all | bytes 8388608 | tf_op jit(solution)/shard_map/all_to_all | solution.py:127
  497.5 2.8 gather_fusion.9
  500.3 2.8 gather_fusion.8
  503.1 4.3 fusion.16
  507.4 5.7 fusion.18
  513.1 2.6 broadcast.453
  515.7 2.7 scatter_fusion.2
  518.4 2.6 scatter_fusion.3
  521.0 4.8 copy.107
  525.9 0.0 reduce-scatter.5.cloned.1.call-update
  525.9 80.4 %reduce-scatter.5.cloned.1.call-done = f32[8,1,16,256]{3,2,0,1:T(8,128)} async-done(((f32[8,32,16,256]{3,2,0,1:T(8,128)}), f32[8,1,16,256]{3,2,0,1:T(8,128)}) %reduce-scatter.5.cloned.1.call-update) | async-done | bytes 131088 | tf_op jit(solution)/shard_map/reduce_scatter | solution.py:135
  606.3 0.8 slice.254
  607.2 3.4 collective-permute-start.3
  610.6 2.7 collective-permute-done.3
  613.3 2.8 fusion.30
  (65 shorter events, 1.1 us)
Async XLA Ops:
  7.2 6.0 copy-start
  7.2 243.6 %collective-permute-start = (f32[4,1,16,256]{3,2,1,0:T(8,128)}, f32[4,1,16,256]{3,2,1,0:T(8,128)S(1)}, u32[]{:S(2)}, u32[]{:S(2)}) collective-permute-start(f32[4,1,16,256]{3,2,1,0:T(8,128)} %param.7), channel_id=1, source_target_pairs={{32,0},{64,32},{96,64},{33,1},{65,33},{97,65},{34,2},{66,34},{98,6... | collective-permute-start | bytes 196616 | tf_op jit(solution)/shard_map/ppermute | solution.py:15
  30.1 67.7 %copy-start.4 = (f32[8,3,1,1]{0,1,3,2:T(4,128)S(1)}, f32[8,3,1,1]{0,1,3,2:T(4,128)}, u32[]{:S(2)}) copy-start(f32[8,3,1,1]{0,1,3,2:T(4,128)} %constant.210) | copy-start | bytes 292
  216.9 34.0 %copy-start.3 = (f32[4,1,16,256]{3,2,1,0:T(8,128)S(1)}, f32[4,1,16,256]{3,2,1,0:T(8,128)}, u32[]{:S(2)}) copy-start(f32[4,1,16,256]{3,2,1,0:T(8,128)} %param.7) | copy-start | bytes 196612
  253.5 61.2 %all-to-all-start = ((f32[32,8,1,16,256]{4,3,2,1,0:T(8,128)}), f32[32,8,1,16,256]{4,3,2,1,0:T(8,128)}, u32[]{:S(2)}, u32[]{:S(2)}) async-start(f32[32,8,1,16,256]{4,3,2,1,0:T(8,128)} %stack.4), calls=%async_computation | async-start | bytes 8388608 | tf_op jit(solution)/shard_map/all_to_all | solution.py:127
  261.9 164.1 %reduce-scatter.3.cloned.1.call-start = ((), (), s32[]{:S(2)}) async-start(), calls=%async_computation.4 | async-start | bytes 4325376 | tf_op jit(solution)/shard_map/reduce_scatter | solution.py:135
  343.0 263.4 %reduce-scatter.5.cloned.1.call-start = ((), (), s32[]{:S(2)}) async-start(), calls=%async_computation.5 | async-start | bytes 4325376 | tf_op jit(solution)/shard_map/reduce_scatter | solution.py:135
  426.8 6.1 collective-permute-start.1
  435.2 178.1 %copy-start.2 = (f32[4,1,16,256]{3,2,0,1:T(8,128)}, f32[4,1,16,256]{3,2,0,1:T(8,128)S(1)}, u32[]{:S(2)}) copy-start(f32[4,1,16,256]{3,2,0,1:T(8,128)S(1)} %fusion.31) | copy-start | bytes 196612
  435.2 6.2 collective-permute-start.2
  518.4 97.7 %copy-start.1 = (s32[3,131072]{1,0:T(4,128)S(1)}, s32[3,131072]{1,0:T(4,128)}, u32[]{:S(2)}) copy-start(s32[3,131072]{1,0:T(4,128)} %param.10) | copy-start | bytes 4718596
  607.2 6.1 collective-permute-start.3
Sparse Core Ops, SparseCore 0:
  343.1 82.8 reduce-scatter.2
  526.0 80.2 reduce-scatter.4
